TPU v7x, 256 devices: a whole 4x4x8 slice. The times are simulated.
256 devices in a mesh: chan: 16 (over z, core), rad: 16 (over y, x).
Axes of the slice: x: 4, y: 4, z: 8, core: 2. Of those that a mesh axis runs over, the one named last changes fastest.
Arguments:
- state: float32 [2048, 2, 16, 1536], P('chan', None, None, 'rad'), may hold values from -200 to 200
- coupling: float32 [64, 16, 4, 32, 32], P('chan'), may hold values from -1.1 to 1.1
- fetch_group: int32 [16, 16], replicated, may hold values from 0 to 3
- live_slots: int32 [64], P('chan'), may hold values from 1 to 16, as said below
- radius_one: float32 [16], replicated, may hold values from 1 to 6
- radius_two: float32 [1536], P('rad'), may hold values from 1 to 6
- kinetic_diag: float32 [12, 128, 128], replicated, may hold values from -2 to 5
- kinetic_link: float32 [11, 128, 128], replicated, may hold values from -0.5 to 0.5
Outputs:
- orthogonal: float32 [2048, 2, 16, 1536], P(('chan', 'rad'))
- arnoldi_coeffs: float32 [3], replicated
Inputs may be any that keep to these rules, and one draw needn't show every extreme that they name: `live_slots`: every draw has a block with all 16 slots live.
All inputs are finite; a program needn't handle non-finite values.
Results may differ from a plain program's by a relative error of at most 0.0003.
Values sent between devices are 32-bit elements; how exact they have to be, the bound alone decides.
A program may use at most 128 MiB of HBM per device.

v0:
```python
import jax
import jax.numpy as jnp
from jax import lax
from jax.sharding import PartitionSpec as P

C = 2048
R = 1536


def radial_kernel(radius_one, radius_two, orders):
    nearer = jnp.minimum(radius_one[:, None], radius_two[None, :])
    farther = jnp.maximum(radius_one[:, None], radius_two[None, :])
    powers = jnp.arange(orders).astype(radius_one.dtype)[:, None, None]
    return nearer[None] ** powers / farther[None] ** (powers + 1.0)


def kinetic(field, kinetic_diag, kinetic_link):
    elements = kinetic_diag.shape[0]
    points = kinetic_diag.shape[1]
    rows = field.reshape(-1, elements, points)
    result = jnp.einsum("rep,eqp->req", rows, kinetic_diag, precision=lax.Precision.HIGHEST)
    lower = jnp.einsum("rep,eqp->req", rows[:, :-1], kinetic_link, precision=lax.Precision.HIGHEST)
    upper = jnp.einsum("rep,epq->req", rows[:, 1:], kinetic_link, precision=lax.Precision.HIGHEST)
    result = (
        result + jnp.pad(lower, ((0, 0), (1, 0), (0, 0))) + jnp.pad(upper, ((0, 0), (0, 1), (0, 0)))
    )
    return result.reshape(field.shape)


def coupling_products(state, coupling, fetch_group, live_slots, radius_one, radius_two):
    chan_count = lax.axis_size("chan")
    my_rank = lax.axis_index("chan")
    local_channels = state.shape[0]
    planes = state.shape[1]
    band = state.shape[2]
    radial = state.shape[3]
    groups_here = coupling.shape[0]
    orders = coupling.shape[2]
    block = coupling.shape[3]
    cells = planes * band * radial
    grouped = state.reshape(groups_here, block, cells)
    outgoing = jnp.take(grouped, fetch_group[:, my_rank], axis=0)
    incoming = lax.all_to_all(outgoing, "chan", split_axis=0, concat_axis=0, tiled=True)
    incoming = incoming.reshape(chan_count * block, cells)
    slot_of = (jnp.arange(chan_count, dtype=jnp.int32) - my_rank) % chan_count
    weights = jnp.take(coupling, slot_of, axis=1)
    active = (slot_of[None, :] < live_slots[:, None]).astype(jnp.float32)
    weights = weights * active[:, :, None, None, None]
    matrices = weights.transpose(2, 0, 3, 1, 4).reshape(orders, local_channels, chan_count * block)
    kernel = radial_kernel(radius_one, radius_two, orders)
    kernel = jnp.broadcast_to(kernel[:, None], (orders, planes, band, radial)).reshape(
        orders, cells
    )
    total = jnp.zeros((local_channels, cells), jnp.float32)
    for order in range(orders):
        product = jnp.dot(
            matrices[order],
            incoming,
            precision=lax.Precision.HIGHEST,
            preferred_element_type=jnp.float32,
        )
        total = total + kernel[order] * product
    return total.reshape(state.shape)


def per_device(
    state, coupling, fetch_group, live_slots, radius_one, radius_two, kinetic_diag, kinetic_link
):
    coupled = coupling_products(state, coupling, fetch_group, live_slots, radius_one, radius_two)
    state_here, coupled_here = (
        lax.all_to_all(state, "rad", split_axis=0, concat_axis=3, tiled=True),
        lax.all_to_all(coupled, "rad", split_axis=0, concat_axis=3, tiled=True),
    )
    applied = kinetic(state_here, kinetic_diag, kinetic_link) + coupled_here
    wave_re = applied[:, 1]
    wave_im = -applied[:, 0]
    state_re = state_here[:, 0]
    state_im = state_here[:, 1]
    total_count = 2.0 * C * state.shape[2] * R
    cross_re = jnp.sum(state_re * wave_re + state_im * wave_im)
    cross_im = jnp.sum(state_re * wave_im - state_im * wave_re)
    self_sq = jnp.sum(state_here * state_here)
    cross_re, cross_im, self_sq = lax.psum((cross_re, cross_im, self_sq), ("chan", "rad"))
    proj_re = cross_re / self_sq
    proj_im = cross_im / self_sq
    orth_re = wave_re - (proj_re * state_re - proj_im * state_im)
    orth_im = wave_im - (proj_re * state_im + proj_im * state_re)
    square_mean = (
        lax.psum(jnp.sum(orth_re * orth_re + orth_im * orth_im), ("chan", "rad")) / total_count
    )
    rms = jnp.sqrt(square_mean + 1e-06)
    orthogonal = jnp.stack([orth_re, orth_im], axis=1)
    return (orthogonal, jnp.stack([proj_re, proj_im, rms]))


def solution(mesh):
    placed = (
        P("chan", None, None, "rad"),
        P("chan", None, None, None, None),
        P(),
        P("chan"),
        P(),
        P("rad"),
        P(),
        P(),
    )
    return jax.shard_map(
        per_device,
        mesh=mesh,
        in_specs=placed,
        out_specs=(P(("chan", "rad"), None, None, None), P()),
        check_vma=False,
    )
```

profile of v0, /device:TPU:1, one launch (start us, length us, event | category | flops | bytes accessed | tf_op | source)
XLA Modules:
  0.0 410.5 jit_solution(6286049403578286027)
XLA Ops:
  0.6 0.0 copy-start
  0.6 1.0 fusion.22
  1.6 0.9 and_reduce_fusion
  2.5 3.0 copy.55
  5.5 2.5 reshape.226
  8.0 3.6 gather_fusion.1
  11.7 6.5 %broadcast_select_fusion = f32[16,32,3072]{2,1,0:T(8,128)} fusion(f32[16,32,3072]{2,1,0:T(8,128)} %gather_fusion.1, pred[16]{0:T(512)(128)(4,1)S(1)} %and_reduce_fusion), kind=kLoop, calls=%fused_computation.11 | loop fusion | flops 1572864 | bytes 12582928 | tf_op jit(solution)/shard_map/jit(_take)/select_n | solution.py:42
  18.1 10.0 %all-to-all-start.1 = ((f32[16,32,3072]{2,1,0:T(8,128)}), f32[16,32,3072]{2,1,0:T(8,128)}, u32[]{:S(2)}, u32[]{:S(2)}) async-start(f32[16,32,3072]{2,1,0:T(8,128)} %broadcast_select_fusion), calls=%async_computation.1 | async-start | bytes 12582912 | tf_op jit(solution)/shard_map/all_to_all | solution.py:43
  28.1 0.1 fusion.18
  28.2 5.0 %gather_fusion = f32[16,4,4,32,32]{4,3,2,1,0:T(8,128)} fusion(f32[4,16,4,32,32]{4,3,2,1,0:T(8,128)} %param.9, s32[1024]{0:T(1024)S(1)} %pad_clamp_fusion.1), kind=kCustom, calls=%fused_computation | custom fusion | bytes 2097216 | tf_op jit(solution)/shard_map/jit(_take)/gather | solution.py:46
  33.2 0.1 compare_convert_fusion
  33.3 2.5 fusion
  35.9 1.9 fusion.24
  37.8 0.6 copy.62
  38.4 0.4 squeeze.23
  38.9 0.1 broadcast_minimum_fusion
  39.0 0.1 power_multiply_fusion
  39.1 0.1 broadcast_in_dim.51
  39.2 1.8 copy.64
  41.1 0.4 squeeze.24
  41.5 0.1 broadcast_in_dim.57
  41.5 1.8 copy.65
  43.4 1.1 squeeze.25
  44.5 0.1 broadcast_in_dim.59
  44.6 0.6 copy.66
  45.2 1.1 squeeze.26
  46.3 0.1 broadcast_in_dim.61
  46.3 120.3 %all-to-all-done.1 = f32[16,32,3072]{2,1,0:T(8,128)} async-done(((f32[16,32,3072]{2,1,0:T(8,128)}), f32[16,32,3072]{2,1,0:T(8,128)}, u32[]{:S(2)}, u32[]{:S(2)}) %all-to-all-start.1) | async-done | bytes 6291488 | tf_op jit(solution)/shard_map/all_to_all | solution.py:43
  166.6 6.8 %all-to-all-start = ((f32[128,2,16,96]{3,2,1,0:T(8,128)}), f32[128,2,16,96]{3,2,1,0:T(8,128)S(1)}, u32[]{:S(2)}, u32[]{:S(2)}) async-start(f32[128,2,16,96]{3,2,1,0:T(8,128)} %copy.55), calls=%async_computation | async-start | bytes 4194304 | tf_op jit(solution)/shard_map/all_to_all | solution.py:71
  173.4 5.6 %convolution_multiply_fusion.3 = f32[128,3072]{1,0:T(8,128)S(1)} fusion(f32[128,512]{1,0:T(8,128)S(1)} %squeeze.23, f32[512,3072]{1,0:T(8,128)} %bitcast.8, f32[3072]{0:T(1024)S(1)} %broadcast_in_dim.51), kind=kOutput, calls=%fused_computation.10 | convolution fusion | flops 2416312320 | bytes 8138752 | tf_op jit(solution)/shard_map/dot_general | solution.py:56
  179.0 0.0 copy-start.6
  179.0 5.6 %fusion.3 = f32[128,3072]{1,0:T(8,128)S(1)} fusion(f32[128,3072]{1,0:T(8,128)S(1)} %convolution_multiply_fusion.3, f32[128,512]{1,0:T(8,128)S(1)} %squeeze.24, f32[512,3072]{1,0:T(8,128)} %bitcast.8, f32[3072]{0:T(1024)S(1)} %broadcast_in_dim.57), kind=kOutput, calls=%fused_computation.9 | convolution fusion | flops 2416705536 | bytes 9711616 | tf_op jit(solution)/shard_map/dot_general | solution.py:56
  184.6 5.6 %fusion.2 = f32[128,3072]{1,0:T(8,128)S(1)} fusion(f32[128,3072]{1,0:T(8,128)S(1)} %fusion.3, f32[128,512]{1,0:T(8,128)S(1)} %copy-done.6, f32[512,3072]{1,0:T(8,128)} %bitcast.8, f32[3072]{0:T(1024)S(1)} %broadcast_in_dim.59), kind=kOutput, calls=%fused_computation.7 | convolution fusion | flops 2416705536 | bytes 9711616 | tf_op jit(solution)/shard_map/dot_general | solution.py:56
  190.2 7.3 %fusion.1 = f32[128,3072]{1,0:T(8,128)} fusion(f32[128,3072]{1,0:T(8,128)S(1)} %fusion.2, f32[128,512]{1,0:T(8,128)S(1)} %copy-done.7, f32[512,3072]{1,0:T(8,128)} %bitcast.8, f32[3072]{0:T(1024)S(1)} %broadcast_in_dim.61), kind=kOutput, calls=%fused_computation.5 | convolution fusion | flops 2416705536 | bytes 9711616 | tf_op jit(solution)/shard_map/dot_general | solution.py:56
  197.6 3.0 copy.67
  200.6 3.0 copy.68
  203.6 1.3 copy-done.4
  204.9 6.7 %all-to-all-start.2 = ((f32[128,2,16,96]{3,2,1,0:T(8,128)}), f32[128,2,16,96]{3,2,1,0:T(8,128)}, u32[]{:S(2)}, u32[]{:S(2)}) async-start(f32[128,2,16,96]{3,2,1,0:T(8,128)} %copy.68), calls=%async_computation.2 | async-start | bytes 4194304 | tf_op jit(solution)/shard_map/all_to_all | solution.py:72
  211.7 2.8 copy.56
  214.5 1.4 copy-done.3
  215.8 1.6 reshape.224
  217.5 2.2 all_to_all.37
  219.7 0.0 copy-start.5
  219.7 2.2 copy.57
  221.9 1.5 convolution_bitcast_fusion
  223.4 1.4 convolution_bitcast_fusion.1
  224.8 2.8 fusion.4
  227.6 2.9 copy.61
  230.5 2.6 reshape.225
  233.1 2.7 multiply_reduce_fusion
  235.8 4.0 all-to-all-done.2
  239.8 4.1 %copy.69 = f32[8,2,16,16,96]{4,3,2,1,0:T(8,128)} copy(f32[8,2,16,16,96]{4,2,1,0,3:T(8,128)} %bitcast.14) | data formatting | bytes 3145728 | tf_op jit(solution)/shard_map/all_to_all | solution.py:72
  244.0 3.1 all_to_all.36
  247.0 2.1 add.110
  249.1 0.0 copy-start.1
  249.1 1.1 fusion.8
  250.2 0.0 copy-done.1
  250.3 77.7 %all-reduce.2 = (f32[]{:T(128)}, f32[]{:T(128)}, f32[]{:T(128)}) all-reduce(f32[]{:T(128)} %get-tuple-element.3, f32[]{:T(128)} %multiply_reduce_fusion, f32[]{:T(128)} %get-tuple-element.2), channel_id=1, replica_groups=mesh['chan'=16,'rad'=16] {'chan','rad'}, use_global_device_ids=true, to_apply=%region_5.6 | all-reduce | flops 3 | bytes 24 | tf_op jit(solution)/shard_map/psum | solution.py:83
  330.5 0.0 copy-start.2
  330.5 2.4 fusion.13
  333.0 1.2 subtract_subtract_fusion
  334.2 72.6 %psum.31 = f32[]{:T(128)} all-reduce(f32[]{:T(128)} %fusion.13), channel_id=1, replica_groups=mesh['chan'=16,'rad'=16] {'chan','rad'}, use_global_device_ids=true, to_apply=%region_7.8 | all-reduce | flops 1 | bytes 8 | tf_op jit(solution)/shard_map/psum | solution.py:89
  407.5 2.4 pad_maximum_fusion
  409.9 0.6 pad_maximum_fusion.1
  (26 shorter events, 0.1 us)
Async XLA Ops:
  0.6 224.2 %copy-start = (f32[12,128,128]{2,1,0:T(8,128)S(1)}, f32[12,128,128]{2,1,0:T(8,128)}, u32[]{:S(2)}) copy-start(f32[12,128,128]{2,1,0:T(8,128)} %param.14) | copy-start | bytes 2359300
  18.1 148.5 %all-to-all-start.1 = ((f32[16,32,3072]{2,1,0:T(8,128)}), f32[16,32,3072]{2,1,0:T(8,128)}, u32[]{:S(2)}, u32[]{:S(2)}) async-start(f32[16,32,3072]{2,1,0:T(8,128)} %broadcast_select_fusion), calls=%async_computation.1 | async-start | bytes 12582912 | tf_op jit(solution)/shard_map/all_to_all | solution.py:43
  28.2 5.0 %copy-start.8 = (s32[4]{0:T(128)S(1)}, s32[4]{0:T(128)}, u32[]{:S(2)}) copy-start(s32[4]{0:T(128)} %param.11) | copy-start | bytes 52
  37.8 1.1 copy-start.9
  37.8 1.1 copy-start.10
  166.6 37.0 %all-to-all-start = ((f32[128,2,16,96]{3,2,1,0:T(8,128)}), f32[128,2,16,96]{3,2,1,0:T(8,128)S(1)}, u32[]{:S(2)}, u32[]{:S(2)}) async-start(f32[128,2,16,96]{3,2,1,0:T(8,128)} %copy.55), calls=%async_computation | async-start | bytes 4194304 | tf_op jit(solution)/shard_map/all_to_all | solution.py:71
  179.0 5.6 %copy-start.6 = (f32[128,512]{1,0:T(8,128)S(1)}, f32[128,512]{1,0:T(8,128)}, u32[]{:S(2)}) copy-start(f32[128,512]{1,0:T(8,128)} %squeeze.25) | copy-start | bytes 786436
  184.6 5.6 %copy-start.7 = (f32[128,512]{1,0:T(8,128)S(1)}, f32[128,512]{1,0:T(8,128)}, u32[]{:S(2)}) copy-start(f32[128,512]{1,0:T(8,128)} %squeeze.26) | copy-start | bytes 786436
  203.6 1.3 copy-start.4
  204.9 34.9 %all-to-all-start.2 = ((f32[128,2,16,96]{3,2,1,0:T(8,128)}), f32[128,2,16,96]{3,2,1,0:T(8,128)}, u32[]{:S(2)}, u32[]{:S(2)}) async-start(f32[128,2,16,96]{3,2,1,0:T(8,128)} %copy.68), calls=%async_computation.2 | async-start | bytes 4194304 | tf_op jit(solution)/shard_map/all_to_all | solution.py:72
  214.4 1.4 copy-start.3
  219.7 2.2 copy-start.5
  249.1 1.1 copy-start.1
  330.5 2.4 copy-start.2
where the time goes:
time: 412 us; the launch traced here: 410 us
  blocking collectives  150 us (36%)
  waiting for transfers between devices  124 us (30%)
  local copies, waits for them, and re-layouts  54.6 us (13%)
  matrix products  29.7 us (7%)
  other arithmetic  23.9 us (6%)
  starting transfers between devices  23.5 us (6%)
  between operations  4.18 us (1%)
    all_to_all x1, waiting for transfers between devices, coupling_products(): lax.all_to_all(outgoing, 'chan', split_axis=0, concat_axis=0, tiled=True)  120 us
    psum x1, blocking collectives, per_device(): lax.psum((cross_re, cross_im, self_sq), ('chan', 'rad'))  77.7 us
    psum x1, blocking collectives, per_device(): lax.psum(jnp.sum(orth_re * orth_re + orth_im * orth_im), ('chan', 'rad'))  72.6 us
    dot_general x4, matrix products, coupling_products(): jnp.dot(matrices[order], incoming, precision=lax.Precision.HIGHEST, prefe...  24.1 us
    all_to_all x1, starting transfers between devices, coupling_products(): lax.all_to_all(outgoing, 'chan', split_axis=0, concat_axis=0, tiled=True)  9.98 us
  transfers between devices with their start and end apart: 3, of which 2 were waited for; matrix products, arithmetic and copies ran while one was open for 17% of the time, Pallas kernels for 0%

commit v1 on v0

--- a/solution.py
+++ b/solution.py
@@ -80,7 +80,7 @@
     cross_re = jnp.sum(state_re * wave_re + state_im * wave_im)
     cross_im = jnp.sum(state_re * wave_im - state_im * wave_re)
     self_sq = jnp.sum(state_here * state_here)
-    cross_re, cross_im, self_sq = lax.psum((cross_re, cross_im, self_sq), ("chan", "rad"))
+    cross_re, cross_im, self_sq = lax.psum(lax.psum((cross_re, cross_im, self_sq), "chan"), "rad")
     proj_re = cross_re / self_sq
     proj_im = cross_im / self_sq
     orth_re = wave_re - (proj_re * state_re - proj_im * state_im)

time: 412 us -> 398 us (0.966)
  blocking collectives: 150 us -> 136 us
    psum x1 -> x2, blocking collectives: 77.7 us -> 56.8 us  [the longest x1 29.6 us: per_device(): lax.psum(lax.psum((cross_re, cross_im, self_sq), 'chan'), 'rad')]
    psum x1, blocking collectives: 72.6 us -> 79.7 us  [per_device(): lax.psum(jnp.sum(orth_re * orth_re + orth_im * orth_im), ('chan', 'rad'))]
where the time goes in v1:
time: 398 us; the launch traced here: 397 us
  blocking collectives  136 us (34%)
  waiting for transfers between devices  124 us (31%)
  local copies, waits for them, and re-layouts  54.6 us (14%)
  matrix products  29.7 us (7%)
  other arithmetic  23.9 us (6%)
  starting transfers between devices  23.5 us (6%)
  between operations  4.17 us (1%)
    all_to_all x1, waiting for transfers between devices, coupling_products(): lax.all_to_all(outgoing, 'chan', split_axis=0, concat_axis=0, tiled=True)  120 us
    psum x1, blocking collectives, per_device(): lax.psum(jnp.sum(orth_re * orth_re + orth_im * orth_im), ('chan', 'rad'))  79.7 us
    psum x1, blocking collectives, per_device(): lax.psum(lax.psum((cross_re, cross_im, self_sq), 'chan'), 'rad')  29.6 us
    psum x1, blocking collectives, per_device(): lax.psum((cross_re, cross_im, self_sq), 'chan')  27.2 us
    dot_general x4, matrix products, coupling_products(): jnp.dot(matrices[order], incoming, precision=lax.Precision.HIGHEST, prefe...  24.1 us
    all_to_all x1, starting transfers between devices, coupling_products(): lax.all_to_all(outgoing, 'chan', split_axis=0, concat_axis=0, tiled=True)  9.98 us
  transfers between devices with their start and end apart: 3, of which 2 were waited for; matrix products, arithmetic and copies ran while one was open for 17% of the time, Pallas kernels for 0%

profile of v1, /device:TPU:1, one launch (start us, length us, event | category | flops | bytes accessed | tf_op | source)
XLA Modules:
  0.0 396.6 jit_solution(2488913897957221060)
XLA Ops:
  0.6 0.0 copy-start
  0.6 1.0 fusion.22
  1.6 0.9 and_reduce_fusion
  2.5 3.0 copy.55
  5.5 2.5 reshape.226
  8.0 3.6 gather_fusion.1
  11.7 6.5 %broadcast_select_fusion = f32[16,32,3072]{2,1,0:T(8,128)} fusion(f32[16,32,3072]{2,1,0:T(8,128)} %gather_fusion.1, pred[16]{0:T(512)(128)(4,1)S(1)} %and_reduce_fusion), kind=kLoop, calls=%fused_computation.11 | loop fusion | flops 1572864 | bytes 12582928 | tf_op jit(solution)/shard_map/jit(_take)/select_n | solution.py:42
  18.1 10.0 %all-to-all-start.1 = ((f32[16,32,3072]{2,1,0:T(8,128)}), f32[16,32,3072]{2,1,0:T(8,128)}, u32[]{:S(2)}, u32[]{:S(2)}) async-start(f32[16,32,3072]{2,1,0:T(8,128)} %broadcast_select_fusion), calls=%async_computation.1 | async-start | bytes 12582912 | tf_op jit(solution)/shard_map/all_to_all | solution.py:43
  28.1 0.1 fusion.18
  28.2 5.0 %gather_fusion = f32[16,4,4,32,32]{4,3,2,1,0:T(8,128)} fusion(f32[4,16,4,32,32]{4,3,2,1,0:T(8,128)} %param.9, s32[1024]{0:T(1024)S(1)} %pad_clamp_fusion.1), kind=kCustom, calls=%fused_computation | custom fusion | bytes 2097216 | tf_op jit(solution)/shard_map/jit(_take)/gather | solution.py:46
  33.2 0.1 compare_convert_fusion
  33.3 2.5 fusion
  35.9 1.9 fusion.24
  37.8 0.6 copy.62
  38.4 0.4 squeeze.23
  38.9 0.1 broadcast_minimum_fusion
  39.0 0.1 power_multiply_fusion
  39.1 0.1 broadcast_in_dim.51
  39.2 1.8 copy.64
  41.1 0.4 squeeze.24
  41.5 0.1 broadcast_in_dim.57
  41.5 1.8 copy.65
  43.4 1.1 squeeze.25
  44.5 0.1 broadcast_in_dim.59
  44.6 0.6 copy.66
  45.2 1.1 squeeze.26
  46.3 0.1 broadcast_in_dim.61
  46.3 120.3 %all-to-all-done.1 = f32[16,32,3072]{2,1,0:T(8,128)} async-done(((f32[16,32,3072]{2,1,0:T(8,128)}), f32[16,32,3072]{2,1,0:T(8,128)}, u32[]{:S(2)}, u32[]{:S(2)}) %all-to-all-start.1) | async-done | bytes 6291488 | tf_op jit(solution)/shard_map/all_to_all | solution.py:43
  166.6 6.8 %all-to-all-start = ((f32[128,2,16,96]{3,2,1,0:T(8,128)}), f32[128,2,16,96]{3,2,1,0:T(8,128)S(1)}, u32[]{:S(2)}, u32[]{:S(2)}) async-start(f32[128,2,16,96]{3,2,1,0:T(8,128)} %copy.55), calls=%async_computation | async-start | bytes 4194304 | tf_op jit(solution)/shard_map/all_to_all | solution.py:71
  173.4 5.6 %convolution_multiply_fusion.3 = f32[128,3072]{1,0:T(8,128)S(1)} fusion(f32[128,512]{1,0:T(8,128)S(1)} %squeeze.23, f32[512,3072]{1,0:T(8,128)} %bitcast.8, f32[3072]{0:T(1024)S(1)} %broadcast_in_dim.51), kind=kOutput, calls=%fused_computation.10 | convolution fusion | flops 2416312320 | bytes 8138752 | tf_op jit(solution)/shard_map/dot_general | solution.py:56
  179.0 0.0 copy-start.6
  179.0 5.6 %fusion.3 = f32[128,3072]{1,0:T(8,128)S(1)} fusion(f32[128,3072]{1,0:T(8,128)S(1)} %convolution_multiply_fusion.3, f32[128,512]{1,0:T(8,128)S(1)} %squeeze.24, f32[512,3072]{1,0:T(8,128)} %bitcast.8, f32[3072]{0:T(1024)S(1)} %broadcast_in_dim.57), kind=kOutput, calls=%fused_computation.9 | convolution fusion | flops 2416705536 | bytes 9711616 | tf_op jit(solution)/shard_map/dot_general | solution.py:56
  184.6 5.6 %fusion.2 = f32[128,3072]{1,0:T(8,128)S(1)} fusion(f32[128,3072]{1,0:T(8,128)S(1)} %fusion.3, f32[128,512]{1,0:T(8,128)S(1)} %copy-done.6, f32[512,3072]{1,0:T(8,128)} %bitcast.8, f32[3072]{0:T(1024)S(1)} %broadcast_in_dim.59), kind=kOutput, calls=%fused_computation.7 | convolution fusion | flops 2416705536 | bytes 9711616 | tf_op jit(solution)/shard_map/dot_general | solution.py:56
  190.2 7.3 %fusion.1 = f32[128,3072]{1,0:T(8,128)} fusion(f32[128,3072]{1,0:T(8,128)S(1)} %fusion.2, f32[128,512]{1,0:T(8,128)S(1)} %copy-done.7, f32[512,3072]{1,0:T(8,128)} %bitcast.8, f32[3072]{0:T(1024)S(1)} %broadcast_in_dim.61), kind=kOutput, calls=%fused_computation.5 | convolution fusion | flops 2416705536 | bytes 9711616 | tf_op jit(solution)/shard_map/dot_general | solution.py:56
  197.6 3.0 copy.67
  200.6 3.0 copy.68
  203.6 1.3 copy-done.4
  204.9 6.7 %all-to-all-start.2 = ((f32[128,2,16,96]{3,2,1,0:T(8,128)}), f32[128,2,16,96]{3,2,1,0:T(8,128)}, u32[]{:S(2)}, u32[]{:S(2)}) async-start(f32[128,2,16,96]{3,2,1,0:T(8,128)} %copy.68), calls=%async_computation.2 | async-start | bytes 4194304 | tf_op jit(solution)/shard_map/all_to_all | solution.py:72
  211.7 2.8 copy.56
  214.5 1.4 copy-done.3
  215.8 1.6 reshape.224
  217.5 2.2 all_to_all.37
  219.7 0.0 copy-start.5
  219.7 2.2 copy.57
  221.9 1.5 convolution_bitcast_fusion
  223.4 1.4 convolution_bitcast_fusion.1
  224.8 2.8 fusion.4
  227.6 2.9 copy.61
  230.5 2.6 reshape.225
  233.1 2.7 multiply_reduce_fusion
  235.8 4.0 %all-to-all-done.2 = f32[128,2,16,96]{3,2,1,0:T(8,128)} async-done(((f32[128,2,16,96]{3,2,1,0:T(8,128)}), f32[128,2,16,96]{3,2,1,0:T(8,128)}, u32[]{:S(2)}, u32[]{:S(2)}) %all-to-all-start.2) | async-done | bytes 1572896 | tf_op jit(solution)/shard_map/all_to_all | solution.py:72
  239.8 4.1 %copy.69 = f32[8,2,16,16,96]{4,3,2,1,0:T(8,128)} copy(f32[8,2,16,16,96]{4,2,1,0,3:T(8,128)} %bitcast.14) | data formatting | bytes 3145728 | tf_op jit(solution)/shard_map/all_to_all | solution.py:72
  244.0 3.1 all_to_all.36
  247.0 2.1 add.116
  249.1 0.0 copy-start.1
  249.1 1.1 fusion.8
  250.2 0.0 copy-done.1
  250.3 27.2 %all-reduce.3 = (f32[]{:T(128)}, f32[]{:T(128)}, f32[]{:T(128)}) all-reduce(f32[]{:T(128)} %get-tuple-element.3, f32[]{:T(128)} %multiply_reduce_fusion, f32[]{:T(128)} %get-tuple-element.2), channel_id=1, replica_groups=mesh['chan'=16,'rad'=16] {'chan'}, use_global_device_ids=true, to_apply=%region_7.8 | all-reduce | flops 3 | bytes 24 | tf_op jit(solution)/shard_map/psum | solution.py:83
  277.5 29.6 %all-reduce.2 = (f32[]{:T(128)}, f32[]{:T(128)}, f32[]{:T(128)}) all-reduce(f32[]{:T(128)} %get-tuple-element.7, f32[]{:T(128)} %get-tuple-element.8, f32[]{:T(128)} %get-tuple-element.9), channel_id=1, replica_groups=mesh['chan'=16,'rad'=16] {'rad'}, use_global_device_ids=true, to_apply=%region_8.9 | all-reduce | flops 3 | bytes 24 | tf_op jit(solution)/shard_map/psum | solution.py:83
  309.6 2.4 fusion.13
  312.0 1.2 subtract_subtract_fusion
  313.2 79.7 %psum.55 = f32[]{:T(128)} all-reduce(f32[]{:T(128)} %fusion.13), channel_id=1, replica_groups=mesh['chan'=16,'rad'=16] {'chan','rad'}, use_global_device_ids=true, to_apply=%region_10.11 | all-reduce | flops 1 | bytes 8 | tf_op jit(solution)/shard_map/psum | solution.py:89
  393.6 2.4 pad_maximum_fusion
  396.0 0.6 pad_maximum_fusion.1
  (27 shorter events, 0.1 us)
Async XLA Ops:
  0.6 224.2 %copy-start = (f32[12,128,128]{2,1,0:T(8,128)S(1)}, f32[12,128,128]{2,1,0:T(8,128)}, u32[]{:S(2)}) copy-start(f32[12,128,128]{2,1,0:T(8,128)} %param.14) | copy-start | bytes 2359300
  18.1 148.5 %all-to-all-start.1 = ((f32[16,32,3072]{2,1,0:T(8,128)}), f32[16,32,3072]{2,1,0:T(8,128)}, u32[]{:S(2)}, u32[]{:S(2)}) async-start(f32[16,32,3072]{2,1,0:T(8,128)} %broadcast_select_fusion), calls=%async_computation.1 | async-start | bytes 12582912 | tf_op jit(solution)/shard_map/all_to_all | solution.py:43
  28.2 5.0 %copy-start.8 = (s32[4]{0:T(128)S(1)}, s32[4]{0:T(128)}, u32[]{:S(2)}) copy-start(s32[4]{0:T(128)} %param.11) | copy-start | bytes 52
  37.8 1.1 copy-start.9
  37.8 1.1 copy-start.10
  166.6 37.0 %all-to-all-start = ((f32[128,2,16,96]{3,2,1,0:T(8,128)}), f32[128,2,16,96]{3,2,1,0:T(8,128)S(1)}, u32[]{:S(2)}, u32[]{:S(2)}) async-start(f32[128,2,16,96]{3,2,1,0:T(8,128)} %copy.55), calls=%async_computation | async-start | bytes 4194304 | tf_op jit(solution)/shard_map/all_to_all | solution.py:71
  179.0 5.6 %copy-start.6 = (f32[128,512]{1,0:T(8,128)S(1)}, f32[128,512]{1,0:T(8,128)}, u32[]{:S(2)}) copy-start(f32[128,512]{1,0:T(8,128)} %squeeze.25) | copy-start | bytes 786436
  184.6 5.6 %copy-start.7 = (f32[128,512]{1,0:T(8,128)S(1)}, f32[128,512]{1,0:T(8,128)}, u32[]{:S(2)}) copy-start(f32[128,512]{1,0:T(8,128)} %squeeze.26) | copy-start | bytes 786436
  203.6 1.3 copy-start.4
  204.9 34.9 %all-to-all-start.2 = ((f32[128,2,16,96]{3,2,1,0:T(8,128)}), f32[128,2,16,96]{3,2,1,0:T(8,128)}, u32[]{:S(2)}, u32[]{:S(2)}) async-start(f32[128,2,16,96]{3,2,1,0:T(8,128)} %copy.68), calls=%async_computation.2 | async-start | bytes 4194304 | tf_op jit(solution)/shard_map/all_to_all | solution.py:72
  214.4 1.4 copy-start.3
  219.7 2.2 copy-start.5
  249.1 1.1 copy-start.1
  309.6 2.4 copy-start.2
